TPU v7x, 32 devices: a whole 2x2x4 slice. The times are simulated.
32 devices in a mesh: grp: 2 (over y), pipe: 8 (over z, x), head: 2 (over core).
Axes of the slice: x: 2, y: 2, z: 4, core: 2. Of those that a mesh axis runs over, the one named last changes fastest.
Arguments:
- queries: bfloat16 [512, 64, 128], P(('grp', 'pipe'), 'head'), parts along dimension 0, may hold values from -10 to 10
- slice_own_keys: bfloat16 [512, 4, 128], P(('grp', 'pipe'), 'head'), parts along dimension 0, may hold values from -6 to 6
- slice_own_values: bfloat16 [512, 4, 128], P(('grp', 'pipe'), 'head'), parts along dimension 0, may hold values from -6 to 6
- cache_keys: bfloat16 [1664, 4, 128], P(('grp', 'pipe'), 'head'), parts along dimension 0, may hold values from -8 to 8
- context_value_rows: bfloat16 [1664, 4, 128], P(('grp', 'pipe'), 'head'), parts along dimension 0, may hold values from -6 to 6
- prefix_len: int32 [16], P('grp'), parts along dimension 0, may hold values from 1 to 832, as said below
Outputs:
- advanced: bfloat16 [512, 64, 128], P(('grp', 'pipe'), 'head'), parts along dimension 0
There are 2 independent parts, one for each index of `grp`. A program takes and returns all parts, laid end to end along the dimension named above; each array names one. Nothing has to cross between parts.
Inputs may be any that keep to these rules, and one draw needn't show every extreme that they name: prefix_len[p] lies in ((8 - 1 - p) * 104, (8 - p) * 104]; prefix_len[0] is 832 and the last section's is 1.
All inputs are finite; a program needn't handle non-finite values.
Results may differ from a plain program's by a relative error of at most 0.012.
Values may be sent and summed in bfloat16 or wider, within the bound.
No kernel may reach another device: no remote copies, remote signals or barrier semaphores. Data moves between devices by JAX's collectives and lax.ppermute only.
A program may use at most 64 MiB of HBM per device.

v0:
```python
import functools
import math

import jax
import jax.numpy as jnp
from jax import lax
from jax.experimental import pallas as pl
from jax.experimental.pallas import tpu as pltpu
from jax.sharding import PartitionSpec as P


floor_value = -1e30
unrolled_sections = 16


def passed_along(value, axis, steps):
    count = lax.axis_size(axis)
    pairs = [(source, (source + steps) % count) for source in range(count)]
    return lax.ppermute(value, axis, pairs)


def attend_kernel(
    scale, groups, chunk, prefix_ref, even_ref, odd_ref, own_ref, *refs
):
    block_refs, out_ref = refs[:-1], refs[-1]
    own_index = lax.axis_index("pipe")
    sections = len(block_refs)
    odd = lax.rem(own_index, 2) == 1
    section = lax.rem(own_index + sections - 1, sections)
    column = lax.broadcasted_iota(jnp.int32, (1, sections), 1)
    prefix = jnp.where(column == section, prefix_ref[...].astype(jnp.float32), 0.0)
    prefix = jnp.sum(prefix, axis=1, keepdims=True).astype(jnp.int32)
    slice_rows, head_count, head_width = out_ref.shape
    per_group = head_count // groups
    block_rows = block_refs[0].shape[1]
    contract = (((1,), (1,)), ((), ()))

    def attend_blocks(masks):
        context = len(masks) * block_rows
        keys_total = context + slice_rows
        position = lax.broadcasted_iota(jnp.int32, (1, keys_total), 1)
        limit = jnp.full((1, keys_total), keys_total, jnp.int32)
        for mask in masks:
            first_key = lax.bitwise_xor(own_index, mask) * block_rows
            stop = jnp.minimum(prefix - first_key, block_rows) + mask * block_rows
            limit = jnp.where(position // block_rows == mask, stop, limit)
        bias = jnp.where(position < limit, 0.0, floor_value)
        for group in range(groups):
            heads = pl.ds(group * per_group, per_group)
            keys = jnp.concatenate(
                [block_refs[mask][group] for mask in masks] + [own_ref[group]], axis=0
            )
            values = jnp.concatenate(
                [block_refs[mask][groups + group] for mask in masks] + [own_ref[groups + group]],
                axis=0,
            )
            for first in range(0, slice_rows, chunk):
                tokens = pl.ds(first, chunk)
                rows = chunk * per_group
                query = jnp.where(odd, odd_ref[tokens, heads, :], even_ref[tokens, heads, :])
                query = query.reshape(rows, head_width)
                scores = lax.dot_general(
                    query, keys, contract, preferred_element_type=jnp.float32
                )
                key_index = lax.broadcasted_iota(jnp.int32, (rows, keys_total), 1) - context
                row_index = lax.broadcasted_iota(jnp.int32, (rows, keys_total), 0) // per_group
                scores = jnp.where(key_index <= row_index + first, scores + bias, floor_value)
                row_max = jnp.max(scores, axis=1, keepdims=True)
                weights = jnp.exp2((scores - row_max) * scale)
                total = jnp.sum(weights, axis=1, keepdims=True)
                weighted = jnp.dot(
                    weights.astype(jnp.bfloat16), values, preferred_element_type=jnp.float32
                )
                out_ref[tokens, heads, :] = (
                    (weighted / total).astype(jnp.bfloat16).reshape(chunk, per_group, head_width)
                )

    @pl.when(own_index == 0)
    def _():
        attend_blocks(range(1))

    @pl.when(own_index != 0)
    def _():
        attend_blocks(range(sections))


def attend(prefix_len, even_query, odd_query, own, blocks, groups):
    slice_rows, head_count, head_width = even_query.shape
    rows = slice_rows * head_count
    vmem = pl.BlockSpec(memory_space=pltpu.VMEM)
    keys = sum(block.shape[1] for block in blocks)
    scale = math.log2(math.e) / math.sqrt(head_width)
    return pl.pallas_call(
        functools.partial(attend_kernel, scale, groups, slice_rows),
        out_shape=jax.ShapeDtypeStruct(even_query.shape, jnp.bfloat16),
        in_specs=[vmem] * (4 + len(blocks)),
        out_specs=vmem,
        compiler_params=pltpu.CompilerParams(vmem_limit_bytes=24 << 20),
        cost_estimate=pl.CostEstimate(
            flops=4 * keys * rows * head_width,
            bytes_accessed=4 * rows * head_width,
            transcendentals=keys * rows,
        ),
        name="attend",
    )(prefix_len.reshape(1, -1), even_query, odd_query, own, *blocks)


def block_scores(grouped, key_block, factor):
    return (
        jnp.einsum("sghd,kgd->gkhs", grouped, key_block, preferred_element_type=jnp.float32)
        * factor
    )


def to_rows(statistic):
    return jnp.transpose(statistic, (2, 0, 1))[..., None]


def absorb(running, scores, value_block, visible):
    weighted, running_max, running_sum = running
    block_max = jnp.max(jnp.where(visible, scores, floor_value), axis=1)
    new_max = jnp.maximum(running_max, block_max)
    weights = jnp.where(visible, jnp.exp(scores - new_max[:, None]), 0.0)
    rescale = jnp.exp(running_max - new_max)
    added = jnp.einsum(
        "gkhs,kgd->sghd",
        weights.astype(jnp.bfloat16),
        value_block,
        preferred_element_type=jnp.float32,
    )
    return (
        weighted * to_rows(rescale) + added,
        new_max,
        running_sum * rescale + jnp.sum(weights, axis=1),
    )


def cache_range(
    running, grouped, whole_keys, whole_values, start_key, stop_key, block_rows, factor
):

    def absorb_block(block_index, carried):
        first_key = block_index * block_rows
        key_block = lax.dynamic_slice_in_dim(whole_keys, first_key, block_rows, 0)
        value_block = lax.dynamic_slice_in_dim(whole_values, first_key, block_rows, 0)
        position = first_key + lax.broadcasted_iota(jnp.int32, (1, block_rows, 1, 1), 1)
        visible = (position >= start_key) & (position < stop_key)
        return absorb(carried, block_scores(grouped, key_block, factor), value_block, visible)

    return lax.fori_loop(
        start_key // block_rows, (stop_key + block_rows - 1) // block_rows, absorb_block, running
    )


def gathered_shards(
    queries, slice_own_keys, slice_own_values, cache_keys, context_value_rows, prefix_len
):
    slice_rows, head_count, head_width = queries.shape
    groups = slice_own_keys.shape[1]
    per_group = head_count // groups
    grouped = queries.reshape(slice_rows, groups, per_group, head_width)
    factor = 1.0 / math.sqrt(head_width)
    initial = (
        jnp.zeros((slice_rows, groups, per_group, head_width), jnp.float32),
        jnp.full((groups, per_group, slice_rows), floor_value, jnp.float32),
        jnp.zeros((groups, per_group, slice_rows), jnp.float32),
    )
    key_index = lax.broadcasted_iota(jnp.int32, (1, slice_rows, 1, slice_rows), 1)
    row_index = lax.broadcasted_iota(jnp.int32, (1, slice_rows, 1, slice_rows), 3)
    running = absorb(
        initial,
        block_scores(grouped, slice_own_keys, factor),
        slice_own_values,
        key_index <= row_index,
    )
    whole_keys = lax.all_gather(cache_keys, "pipe", axis=0, tiled=True)
    whole_values = lax.all_gather(context_value_rows, "pipe", axis=0, tiled=True)
    block_rows = math.gcd(whole_keys.shape[0], 512)
    own_prefix = prefix_len[lax.axis_index("pipe")]
    weighted, _, running_sum = cache_range(
        running, grouped, whole_keys, whole_values, 0, own_prefix, block_rows, factor
    )
    result = (weighted / to_rows(running_sum)).astype(jnp.bfloat16).reshape(queries.shape)
    return passed_along(result, "pipe", 1)


def gather_plan(sections):
    every = range(sections)
    top = sections // 2

    def rank(mask):
        if mask.bit_count() > 1:
            return mask.bit_count(), -mask
        return 1, 0 if mask == top else mask

    moves = []
    for mask in sorted(range(1, sections), key=rank):
        swap = [(device, device ^ (mask & -mask)) for device in every]
        moves.append((f"m{mask}", f"m{mask & (mask - 1)}", swap))
    singles = sections.bit_length() - 1
    neighbours = [(device, device ^ 1) for device in every]
    ring = [(device, (device + 1) % sections) for device in every]
    onward = [(d, d ^ 2 if d % 2 else (d + 2) % sections) for d in every]
    return [
        ("near_query", "query", neighbours),
        *moves[:singles],
        ("near_own", "own", ring),
        *moves[singles:-1],
        ("even_query", "near_query", onward),
        moves[-1],
    ]


def packed(keys, values):
    return jnp.concatenate([jnp.transpose(keys, (1, 0, 2)), jnp.transpose(values, (1, 0, 2))])


def swapped_shards(
    queries, slice_own_keys, slice_own_values, cache_keys, context_value_rows, prefix_len
):
    groups = slice_own_keys.shape[1]
    sections = lax.axis_size("pipe")

    held = {
        "query": queries,
        "own": packed(slice_own_keys, slice_own_values),
        "m0": packed(cache_keys, context_value_rows),
    }
    for name, source, pairs in gather_plan(sections):
        held[name] = lax.ppermute(held[source], "pipe", pairs)
    blocks = [held[f"m{mask}"] for mask in range(sections)]
    return attend(
        prefix_len, held["even_query"], held["near_query"], held["near_own"], blocks, groups
    )


def solution(mesh):
    sections = mesh.shape["pipe"]
    unrolled = 4 <= sections <= unrolled_sections and sections & (sections - 1) == 0
    shards = swapped_shards if unrolled else gathered_shards
    in_specs = (
        P(("grp", "pipe"), "head", None),
        P(("grp", "pipe"), "head", None),
        P(("grp", "pipe"), "head", None),
        P(("grp", "pipe"), "head", None),
        P(("grp", "pipe"), "head", None),
        P("grp"),
    )
    out_specs = P(("grp", "pipe"), "head", None)
    return jax.shard_map(shards, mesh=mesh, in_specs=in_specs, out_specs=out_specs, check_vma=False)
```

profile of v0, /device:TPU:0, one launch (start us, length us, event | category | flops | bytes accessed | tf_op | source)
XLA Modules:
  0.0 31.8 jit_solution(5931441183576146111)
XLA Ops:
  0.0 3.0 %collective-permute-start = (bf16[32,32,128]{2,1,0:T(8,128)(2,1)}, bf16[32,32,128]{2,1,0:T(8,128)(2,1)S(1)}, u32[]{:S(2)}, u32[]{:S(2)}) collective-permute-start(bf16[32,32,128]{2,1,0:T(8,128)(2,1)} %param.6), channel_id=1, source_target_pairs={{0,2},{2,0},{4,6},{6,4},{8,10},{10,8},{12,14},{14,12},{1,3},{3,1},... | collective-permute-start | bytes 786440 | tf_op jit(solution)/shard_map/ppermute | solution.py:230
  3.0 0.8 %copy_bitcast_fusion = (bf16[2,104,128]{2,1,0:T(8,128)(2,1)S(1)}, bf16[2,104,128]{2,1,0:T(8,128)(2,1)S(1)}) fusion(bf16[104,2,128]{2,1,0:T(2,128)(2,1)} %param.10, bf16[104,2,128]{2,1,0:T(2,128)(2,1)} %param.9), kind=kLoop, calls=%fused_computation.1 | loop fusion | bytes 212992 | tf_op jit(solution)/shard_map/transpose | solution.py:215
  3.8 0.0 copy-start.1
  3.8 0.0 copy-start.2
  3.9 2.7 %collective-permute-start.6 = (bf16[4,104,128]{2,1,0:T(8,128)(2,1)S(1)}, bf16[4,104,128]{2,1,0:T(8,128)(2,1)S(1)}, u32[]{:S(2)}, u32[]{:S(2)}) collective-permute-start(bf16[4,104,128]{2,1,0:T(8,128)(2,1)S(1)} %pad_maximum_fusion.refs_0_), channel_id=1, source_target_pairs={{0,8},{2,10},{4,12},{6,14},{8,0},{10,2},{12,4},{14,6},{1,9},{3,11}... | collective-permute-start | bytes 319496 | tf_op jit(solution)/shard_map/ppermute | solution.py:230
  6.5 1.6 %collective-permute-start.4 = (bf16[4,104,128]{2,1,0:T(8,128)(2,1)S(1)}, bf16[4,104,128]{2,1,0:T(8,128)(2,1)S(1)}, u32[]{:S(2)}, u32[]{:S(2)}) collective-permute-start(bf16[4,104,128]{2,1,0:T(8,128)(2,1)S(1)} %pad_maximum_fusion.refs_0_), channel_id=1, source_target_pairs={{0,4},{2,6},{4,0},{6,2},{8,12},{10,14},{12,8},{14,10},{1,5},{3,7},... | collective-permute-start | bytes 319496 | tf_op jit(solution)/shard_map/ppermute | solution.py:230
  8.1 1.4 %collective-permute-done.odd_ref = bf16[32,32,128]{2,1,0:T(8,128)(2,1)S(1)} collective-permute-done((bf16[32,32,128]{2,1,0:T(8,128)(2,1)}, bf16[32,32,128]{2,1,0:T(8,128)(2,1)S(1)}, u32[]{:S(2)}, u32[]{:S(2)}) %collective-permute-start) | collective-permute-done | bytes 262176 | tf_op jit(solution)/shard_map/ppermute | solution.py:230
  9.5 1.8 %collective-permute-start.1 = (bf16[32,32,128]{2,1,0:T(8,128)(2,1)S(1)}, bf16[32,32,128]{2,1,0:T(8,128)(2,1)S(1)}, u32[]{:S(2)}, u32[]{:S(2)}) collective-permute-start(bf16[32,32,128]{2,1,0:T(8,128)(2,1)S(1)} %collective-permute-done.odd_ref), channel_id=1, source_target_pairs={{0,4},{2,6},{4,8},{6,2},{8,12},{10,14},{12,0},{14,10},{1,5},{3,7},... | collective-permute-start | bytes 786440 | tf_op jit(solution)/shard_map/ppermute | solution.py:230
  11.3 0.0 copy-done.1
  11.3 0.0 copy-done.2
  11.3 0.2 collective-permute-done.6.refs_4_
  11.5 1.4 %collective-permute-start.8 = (bf16[4,104,128]{2,1,0:T(8,128)(2,1)S(1)}, bf16[4,104,128]{2,1,0:T(8,128)(2,1)S(1)}, u32[]{:S(2)}, u32[]{:S(2)}) collective-permute-start(bf16[4,104,128]{2,1,0:T(8,128)(2,1)S(1)} %collective-permute-done.6.refs_4_), channel_id=1, source_target_pairs={{0,4},{2,6},{4,0},{6,2},{8,12},{10,14},{12,8},{14,10},{1,5},{3,7},... | collective-permute-start | bytes 319496 | tf_op jit(solution)/shard_map/ppermute | solution.py:230
  13.0 0.0 copy-start
  13.0 0.4 %collective-permute-start.2 = (bf16[4,32,128]{2,1,0:T(8,128)(2,1)S(1)}, bf16[4,32,128]{2,1,0:T(8,128)(2,1)S(1)}, u32[]{:S(2)}, u32[]{:S(2)}) collective-permute-start(bf16[4,32,128]{2,1,0:T(8,128)(2,1)S(1)} %pad_maximum_fusion.1), channel_id=1, source_target_pairs={{0,2},{2,4},{4,6},{6,8},{8,10},{10,12},{12,14},{14,0},{1,3},{3,5},... | collective-permute-start | bytes 98312 | tf_op jit(solution)/shard_map/ppermute | solution.py:230
  13.4 1.7 %collective-permute-start.3 = (bf16[4,104,128]{2,1,0:T(8,128)(2,1)S(1)}, bf16[4,104,128]{2,1,0:T(8,128)(2,1)S(1)}, u32[]{:S(2)}, u32[]{:S(2)}) collective-permute-start(bf16[4,104,128]{2,1,0:T(8,128)(2,1)S(1)} %pad_maximum_fusion.refs_0_), channel_id=1, source_target_pairs={{0,2},{2,0},{4,6},{6,4},{8,10},{10,8},{12,14},{14,12},{1,3},{3,1},... | collective-permute-start | bytes 319496 | tf_op jit(solution)/shard_map/ppermute | solution.py:230
  15.0 7.8 %collective-permute-done.2.own_ref = bf16[4,32,128]{2,1,0:T(8,128)(2,1)S(1)} collective-permute-done((bf16[4,32,128]{2,1,0:T(8,128)(2,1)S(1)}, bf16[4,32,128]{2,1,0:T(8,128)(2,1)S(1)}, u32[]{:S(2)}, u32[]{:S(2)}) %collective-permute-start.2) | collective-permute-done | bytes 32800 | tf_op jit(solution)/shard_map/ppermute | solution.py:230
  22.9 0.0 collective-permute-start.7
  22.9 0.0 collective-permute-done.4.refs_2_
  22.9 2.0 %collective-permute-start.5 = (bf16[4,104,128]{2,1,0:T(8,128)(2,1)S(1)}, bf16[4,104,128]{2,1,0:T(8,128)(2,1)S(1)}, u32[]{:S(2)}, u32[]{:S(2)}) collective-permute-start(bf16[4,104,128]{2,1,0:T(8,128)(2,1)S(1)} %collective-permute-done.4.refs_2_), channel_id=1, source_target_pairs={{0,2},{2,0},{4,6},{6,4},{8,10},{10,8},{12,14},{14,12},{1,3},{3,1},... | collective-permute-start | bytes 319496 | tf_op jit(solution)/shard_map/ppermute | solution.py:230
  24.9 0.0 collective-permute-done.8.refs_6_
  24.9 0.1 collective-permute-start.9
  25.0 0.0 collective-permute-done.3.refs_1_
  25.0 2.9 %collective-permute-done.7.refs_5_ = bf16[4,104,128]{2,1,0:T(8,128)(2,1)S(1)} collective-permute-done((bf16[4,104,128]{2,1,0:T(8,128)(2,1)S(1)}, bf16[4,104,128]{2,1,0:T(8,128)(2,1)S(1)}, u32[]{:S(2)}, u32[]{:S(2)}) %collective-permute-start.7) | collective-permute-done | bytes 106528 | tf_op jit(solution)/shard_map/ppermute | solution.py:230
  27.8 1.1 %collective-permute-done.5.refs_3_ = bf16[4,104,128]{2,1,0:T(8,128)(2,1)S(1)} collective-permute-done((bf16[4,104,128]{2,1,0:T(8,128)(2,1)S(1)}, bf16[4,104,128]{2,1,0:T(8,128)(2,1)S(1)}, u32[]{:S(2)}, u32[]{:S(2)}) %collective-permute-start.5) | collective-permute-done | bytes 106528 | tf_op jit(solution)/shard_map/ppermute | solution.py:230
  29.0 1.1 %collective-permute-done.9.refs_7_ = bf16[4,104,128]{2,1,0:T(8,128)(2,1)S(1)} collective-permute-done((bf16[4,104,128]{2,1,0:T(8,128)(2,1)S(1)}, bf16[4,104,128]{2,1,0:T(8,128)(2,1)S(1)}, u32[]{:S(2)}, u32[]{:S(2)}) %collective-permute-start.9) | collective-permute-done | bytes 106528 | tf_op jit(solution)/shard_map/ppermute | solution.py:230
  30.1 0.0 collective-permute-done.1.even_ref
  30.1 0.0 copy-done
  30.1 1.6 %attend.1 = bf16[32,32,128]{2,1,0:T(8,128)(2,1)} custom-call(s32[1,8]{1,0:T(1,128)S(1)} %bitcast.9, bf16[32,32,128]{2,1,0:T(8,128)(2,1)S(1)} %collective-permute-done.1.even_ref, bf16[32,32,128]{2,1,0:T(8,128)(2,1)S(1)} %collective-permute-done.odd_ref, bf16[4,32,128]{2,1,0:T(8,128)(2,1)S(1)} %collective-permute-done.2.own_ref, ...), custom_call_target="tpu_custom_call" | custom-call | flops 436207616 | bytes 524288 | tf_op jit(solution)/shard_map/attend/pallas_call | solution.py:93
  (3 shorter events, 0.0 us)
Async XLA Ops:
  0.0 9.5 %collective-permute-start = (bf16[32,32,128]{2,1,0:T(8,128)(2,1)}, bf16[32,32,128]{2,1,0:T(8,128)(2,1)S(1)}, u32[]{:S(2)}, u32[]{:S(2)}) collective-permute-start(bf16[32,32,128]{2,1,0:T(8,128)(2,1)} %param.6), channel_id=1, source_target_pairs={{0,2},{2,0},{4,6},{6,4},{8,10},{10,8},{12,14},{14,12},{1,3},{3,1},... | collective-permute-start | bytes 786440 | tf_op jit(solution)/shard_map/ppermute | solution.py:230
  3.8 7.5 %copy-start.1 = (bf16[32,2,128]{2,1,0:T(2,128)(2,1)S(1)}, bf16[32,2,128]{2,1,0:T(2,128)(2,1)}, u32[]{:S(2)}) copy-start(bf16[32,2,128]{2,1,0:T(2,128)(2,1)} %param.8) | copy-start | bytes 49156
  3.8 7.5 %copy-start.2 = (bf16[32,2,128]{2,1,0:T(2,128)(2,1)S(1)}, bf16[32,2,128]{2,1,0:T(2,128)(2,1)}, u32[]{:S(2)}) copy-start(bf16[32,2,128]{2,1,0:T(2,128)(2,1)} %param.7) | copy-start | bytes 49156
  3.9 7.7 %collective-permute-start.6 = (bf16[4,104,128]{2,1,0:T(8,128)(2,1)S(1)}, bf16[4,104,128]{2,1,0:T(8,128)(2,1)S(1)}, u32[]{:S(2)}, u32[]{:S(2)}) collective-permute-start(bf16[4,104,128]{2,1,0:T(8,128)(2,1)S(1)} %pad_maximum_fusion.refs_0_), channel_id=1, source_target_pairs={{0,8},{2,10},{4,12},{6,14},{8,0},{10,2},{12,4},{14,6},{1,9},{3,11}... | collective-permute-start | bytes 319496 | tf_op jit(solution)/shard_map/ppermute | solution.py:230
  6.5 16.3 %collective-permute-start.4 = (bf16[4,104,128]{2,1,0:T(8,128)(2,1)S(1)}, bf16[4,104,128]{2,1,0:T(8,128)(2,1)S(1)}, u32[]{:S(2)}, u32[]{:S(2)}) collective-permute-start(bf16[4,104,128]{2,1,0:T(8,128)(2,1)S(1)} %pad_maximum_fusion.refs_0_), channel_id=1, source_target_pairs={{0,4},{2,6},{4,0},{6,2},{8,12},{10,14},{12,8},{14,10},{1,5},{3,7},... | collective-permute-start | bytes 319496 | tf_op jit(solution)/shard_map/ppermute | solution.py:230
  9.5 20.7 %collective-permute-start.1 = (bf16[32,32,128]{2,1,0:T(8,128)(2,1)S(1)}, bf16[32,32,128]{2,1,0:T(8,128)(2,1)S(1)}, u32[]{:S(2)}, u32[]{:S(2)}) collective-permute-start(bf16[32,32,128]{2,1,0:T(8,128)(2,1)S(1)} %collective-permute-done.odd_ref), channel_id=1, source_target_pairs={{0,4},{2,6},{4,8},{6,2},{8,12},{10,14},{12,0},{14,10},{1,5},{3,7},... | collective-permute-start | bytes 786440 | tf_op jit(solution)/shard_map/ppermute | solution.py:230
  11.5 13.4 %collective-permute-start.8 = (bf16[4,104,128]{2,1,0:T(8,128)(2,1)S(1)}, bf16[4,104,128]{2,1,0:T(8,128)(2,1)S(1)}, u32[]{:S(2)}, u32[]{:S(2)}) collective-permute-start(bf16[4,104,128]{2,1,0:T(8,128)(2,1)S(1)} %collective-permute-done.6.refs_4_), channel_id=1, source_target_pairs={{0,4},{2,6},{4,0},{6,2},{8,12},{10,14},{12,8},{14,10},{1,5},{3,7},... | collective-permute-start | bytes 319496 | tf_op jit(solution)/shard_map/ppermute | solution.py:230
  13.0 17.2 %copy-start = (s32[8]{0:T(128)S(1)}, s32[8]{0:T(128)}, u32[]{:S(2)}) copy-start(s32[8]{0:T(128)} %param.11) | copy-start | bytes 100
  13.0 9.9 %collective-permute-start.2 = (bf16[4,32,128]{2,1,0:T(8,128)(2,1)S(1)}, bf16[4,32,128]{2,1,0:T(8,128)(2,1)S(1)}, u32[]{:S(2)}, u32[]{:S(2)}) collective-permute-start(bf16[4,32,128]{2,1,0:T(8,128)(2,1)S(1)} %pad_maximum_fusion.1), channel_id=1, source_target_pairs={{0,2},{2,4},{4,6},{6,8},{8,10},{10,12},{12,14},{14,0},{1,3},{3,5},... | collective-permute-start | bytes 98312 | tf_op jit(solution)/shard_map/ppermute | solution.py:230
  13.4 11.6 %collective-permute-start.3 = (bf16[4,104,128]{2,1,0:T(8,128)(2,1)S(1)}, bf16[4,104,128]{2,1,0:T(8,128)(2,1)S(1)}, u32[]{:S(2)}, u32[]{:S(2)}) collective-permute-start(bf16[4,104,128]{2,1,0:T(8,128)(2,1)S(1)} %pad_maximum_fusion.refs_0_), channel_id=1, source_target_pairs={{0,2},{2,0},{4,6},{6,4},{8,10},{10,8},{12,14},{14,12},{1,3},{3,1},... | collective-permute-start | bytes 319496 | tf_op jit(solution)/shard_map/ppermute | solution.py:230
  22.9 5.0 %collective-permute-start.7 = (bf16[4,104,128]{2,1,0:T(8,128)(2,1)S(1)}, bf16[4,104,128]{2,1,0:T(8,128)(2,1)S(1)}, u32[]{:S(2)}, u32[]{:S(2)}) collective-permute-start(bf16[4,104,128]{2,1,0:T(8,128)(2,1)S(1)} %collective-permute-done.6.refs_4_), channel_id=1, source_target_pairs={{0,2},{2,0},{4,6},{6,4},{8,10},{10,8},{12,14},{14,12},{1,3},{3,1},... | collective-permute-start | bytes 319496 | tf_op jit(solution)/shard_map/ppermute | solution.py:230
  22.9 6.1 %collective-permute-start.5 = (bf16[4,104,128]{2,1,0:T(8,128)(2,1)S(1)}, bf16[4,104,128]{2,1,0:T(8,128)(2,1)S(1)}, u32[]{:S(2)}, u32[]{:S(2)}) collective-permute-start(bf16[4,104,128]{2,1,0:T(8,128)(2,1)S(1)} %collective-permute-done.4.refs_2_), channel_id=1, source_target_pairs={{0,2},{2,0},{4,6},{6,4},{8,10},{10,8},{12,14},{14,12},{1,3},{3,1},... | collective-permute-start | bytes 319496 | tf_op jit(solution)/shard_map/ppermute | solution.py:230
  24.9 5.2 %collective-permute-start.9 = (bf16[4,104,128]{2,1,0:T(8,128)(2,1)S(1)}, bf16[4,104,128]{2,1,0:T(8,128)(2,1)S(1)}, u32[]{:S(2)}, u32[]{:S(2)}) collective-permute-start(bf16[4,104,128]{2,1,0:T(8,128)(2,1)S(1)} %collective-permute-done.8.refs_6_), channel_id=1, source_target_pairs={{0,2},{2,0},{4,6},{6,4},{8,10},{10,8},{12,14},{14,12},{1,3},{3,1},... | collective-permute-start | bytes 319496 | tf_op jit(solution)/shard_map/ppermute | solution.py:230
where the time goes:
time: 31.9 us; the launch traced here: 31.8 us
  starting transfers between devices  14.6 us (46%)
  waiting for transfers between devices  14.6 us (46%)
  Pallas kernels  1.64 us (5%)
  local copies, waits for them, and re-layouts  0.87 us (3%)
    ppermute x10, starting transfers between devices, swapped_shards(): held[name] = lax.ppermute(held[source], 'pipe', pairs)  14.6 us
    ppermute x10, waiting for transfers between devices, swapped_shards(): held[name] = lax.ppermute(held[source], 'pipe', pairs)  14.6 us
    pallas_call x1, Pallas kernels, attend(): pl.pallas_call(functools.partial(attend_kernel, scale, groups, slice_rows...  1.64 us
    transpose x2, local copies, waits for them, and re-layouts, packed(): jnp.transpose(values, (1, 0, 2))  0.86 us
  transfers between devices with their start and end apart: 10, of which 6 were waited for; matrix products, arithmetic and copies ran while one was open for 3% of the time, Pallas kernels for 0%

commit v1 on v0

--- a/solution.py
+++ b/solution.py
@@ -19,90 +19,187 @@
     return lax.ppermute(value, axis, pairs)
 
 
-def attend_kernel(
-    scale, groups, chunk, prefix_ref, even_ref, odd_ref, own_ref, *refs
-):
-    block_refs, out_ref = refs[:-1], refs[-1]
-    own_index = lax.axis_index("pipe")
-    sections = len(block_refs)
-    odd = lax.rem(own_index, 2) == 1
-    section = lax.rem(own_index + sections - 1, sections)
+contract = (((1,), (1,)), ((), ()))
+
+
+def own_prefix(prefix_ref):
+    sections = prefix_ref.shape[1]
+    section = lax.rem(lax.axis_index("pipe") + sections - 1, sections)
     column = lax.broadcasted_iota(jnp.int32, (1, sections), 1)
     prefix = jnp.where(column == section, prefix_ref[...].astype(jnp.float32), 0.0)
-    prefix = jnp.sum(prefix, axis=1, keepdims=True).astype(jnp.int32)
+    return jnp.sum(prefix, axis=1, keepdims=True).astype(jnp.int32)
+
+
+def visible_bias(prefix, masks, block_rows, extra):
+    own_index = lax.axis_index("pipe")
+    total = len(masks) * block_rows + extra
+    position = lax.broadcasted_iota(jnp.int32, (1, total), 1)
+    limit = jnp.full((1, total), total, jnp.int32)
+    for slot, mask in enumerate(masks):
+        first_key = lax.bitwise_xor(own_index, mask) * block_rows
+        stop = jnp.minimum(prefix - first_key, block_rows) + slot * block_rows
+        limit = jnp.where(position // block_rows == slot, stop, limit)
+    return jnp.where(position < limit, 0.0, floor_value)
+
+
+def joined_query(odd, heads, even_ref, odd_ref, ring_ref, slice_rows):
+    relayed = jnp.where(odd, odd_ref[:, heads, :], even_ref[:, heads, :])
+    rest = slice_rows - even_ref.shape[0]
+    return jnp.concatenate([relayed, ring_ref[:rest, heads, :]], axis=0)
+
+
+def early_kernel(scale, groups, masks, prefix_ref, even_ref, odd_ref, ring_ref, *refs):
+    block_refs = dict(zip(masks, refs))
+    weighted_ref, max_ref, sum_ref, hbm_ref, out_ref, sems = refs[len(masks):]
+    own_index = lax.axis_index("pipe")
+    odd = lax.rem(own_index, 2) == 1
+    prefix = own_prefix(prefix_ref)
     slice_rows, head_count, head_width = out_ref.shape
     per_group = head_count // groups
+    rows = slice_rows * per_group
     block_rows = block_refs[0].shape[1]
-    contract = (((1,), (1,)), ((), ()))
-
-    def attend_blocks(masks):
+    rest = slice_rows - even_ref.shape[0]
+
+    def part(group, masks, bias):
+        heads = pl.ds(group * per_group, per_group)
         context = len(masks) * block_rows
-        keys_total = context + slice_rows
-        position = lax.broadcasted_iota(jnp.int32, (1, keys_total), 1)
-        limit = jnp.full((1, keys_total), keys_total, jnp.int32)
-        for mask in masks:
-            first_key = lax.bitwise_xor(own_index, mask) * block_rows
-            stop = jnp.minimum(prefix - first_key, block_rows) + mask * block_rows
-            limit = jnp.where(position // block_rows == mask, stop, limit)
-        bias = jnp.where(position < limit, 0.0, floor_value)
+        keys = [block_refs[mask][group] for mask in masks] + [ring_ref[rest + group]]
+        values = [block_refs[mask][groups + group] for mask in masks] + [ring_ref[rest + groups + group]]
+        query = joined_query(odd, heads, even_ref, odd_ref, ring_ref, slice_rows)
+        scores = lax.dot_general(
+            query.reshape(rows, head_width),
+            jnp.concatenate(keys, axis=0),
+            contract,
+            preferred_element_type=jnp.float32,
+        )
+        key_index = lax.broadcasted_iota(jnp.int32, scores.shape, 1) - context
+        row_index = lax.broadcasted_iota(jnp.int32, scores.shape, 0) // per_group
+        scores = jnp.where(key_index <= row_index, scores + bias, floor_value)
+        row_max = jnp.max(scores, axis=1, keepdims=True)
+        weights = jnp.exp2((scores - row_max) * scale)
+        total = jnp.sum(weights, axis=1, keepdims=True)
+        weighted = jnp.dot(
+            weights.astype(jnp.bfloat16),
+            jnp.concatenate(values, axis=0),
+            preferred_element_type=jnp.float32,
+        )
+        return weighted, row_max, total
+
+    @pl.when(own_index == 0)
+    def _():
+        bias = visible_bias(prefix, masks[:1], block_rows, slice_rows)
+        copies = []
         for group in range(groups):
             heads = pl.ds(group * per_group, per_group)
-            keys = jnp.concatenate(
-                [block_refs[mask][group] for mask in masks] + [own_ref[group]], axis=0
+            weighted, _, total = part(group, masks[:1], bias)
+            result = (weighted / total).astype(jnp.bfloat16)
+            out_ref[:, heads, :] = result.reshape(slice_rows, per_group, head_width)
+            copies.append(
+                pltpu.make_async_copy(
+                    out_ref.at[:, heads, :], hbm_ref.at[:, heads, :], sems.at[group]
+                )
             )
-            values = jnp.concatenate(
-                [block_refs[mask][groups + group] for mask in masks] + [own_ref[groups + group]],
-                axis=0,
-            )
-            for first in range(0, slice_rows, chunk):
-                tokens = pl.ds(first, chunk)
-                rows = chunk * per_group
-                query = jnp.where(odd, odd_ref[tokens, heads, :], even_ref[tokens, heads, :])
-                query = query.reshape(rows, head_width)
-                scores = lax.dot_general(
-                    query, keys, contract, preferred_element_type=jnp.float32
-                )
-                key_index = lax.broadcasted_iota(jnp.int32, (rows, keys_total), 1) - context
-                row_index = lax.broadcasted_iota(jnp.int32, (rows, keys_total), 0) // per_group
-                scores = jnp.where(key_index <= row_index + first, scores + bias, floor_value)
-                row_max = jnp.max(scores, axis=1, keepdims=True)
-                weights = jnp.exp2((scores - row_max) * scale)
-                total = jnp.sum(weights, axis=1, keepdims=True)
-                weighted = jnp.dot(
-                    weights.astype(jnp.bfloat16), values, preferred_element_type=jnp.float32
-                )
-                out_ref[tokens, heads, :] = (
-                    (weighted / total).astype(jnp.bfloat16).reshape(chunk, per_group, head_width)
-                )
-
-    @pl.when(own_index == 0)
-    def _():
-        attend_blocks(range(1))
+            copies[-1].start()
+        for copy in copies:
+            copy.wait()
 
     @pl.when(own_index != 0)
     def _():
-        attend_blocks(range(sections))
-
-
-def attend(prefix_len, even_query, odd_query, own, blocks, groups):
-    slice_rows, head_count, head_width = even_query.shape
+        bias = visible_bias(prefix, masks, block_rows, slice_rows)
+        for group in range(groups):
+            weighted, row_max, total = part(group, masks, bias)
+            weighted_ref[group] = weighted
+            max_ref[group] = jnp.broadcast_to(row_max, (rows, head_width))
+            sum_ref[group] = jnp.broadcast_to(total, (rows, head_width))
+
+
+def late_kernel(scale, groups, masks, prefix_ref, even_ref, odd_ref, ring_ref, *refs):
+    block_refs = refs[: len(masks)]
+    weighted_ref, max_ref, sum_ref, _, hbm_ref, out_ref, sems = refs[len(masks) :]
+    own_index = lax.axis_index("pipe")
+    odd = lax.rem(own_index, 2) == 1
+    slice_rows, head_count, head_width = out_ref.shape
+    per_group = head_count // groups
+    rows = slice_rows * per_group
+    block_rows = block_refs[0].shape[1]
+
+    @pl.when(own_index != 0)
+    def _():
+        bias = visible_bias(own_prefix(prefix_ref), masks, block_rows, 0)
+        copies = []
+        for group in range(groups):
+            heads = pl.ds(group * per_group, per_group)
+            query = joined_query(odd, heads, even_ref, odd_ref, ring_ref, slice_rows)
+            scores = bias + lax.dot_general(
+                query.reshape(rows, head_width),
+                jnp.concatenate([block_ref[group] for block_ref in block_refs], axis=0),
+                contract,
+                preferred_element_type=jnp.float32,
+            )
+            old_max = max_ref[group]
+            new_max = jnp.maximum(old_max, jnp.max(scores, axis=1, keepdims=True))
+            rescale = jnp.exp2((old_max - new_max) * scale)
+            weights = jnp.exp2((scores - new_max[:, :1]) * scale)
+            added = jnp.dot(
+                weights.astype(jnp.bfloat16),
+                jnp.concatenate([block_ref[groups + group] for block_ref in block_refs], axis=0),
+                preferred_element_type=jnp.float32,
+            )
+            total = sum_ref[group] * rescale + jnp.sum(weights, axis=1, keepdims=True)
+            result = ((weighted_ref[group] * rescale + added) / total).astype(jnp.bfloat16)
+            out_ref[:, heads, :] = result.reshape(slice_rows, per_group, head_width)
+            copies.append(
+                pltpu.make_async_copy(
+                    out_ref.at[:, heads, :], hbm_ref.at[:, heads, :], sems.at[group]
+                )
+            )
+            copies[-1].start()
+        for copy in copies:
+            copy.wait()
+
+
+def attend(prefix_len, even_query, odd_query, ring, blocks, late, shape, groups):
+    slice_rows, head_count, head_width = shape
     rows = slice_rows * head_count
     vmem = pl.BlockSpec(memory_space=pltpu.VMEM)
-    keys = sum(block.shape[1] for block in blocks)
+    hbm = pl.BlockSpec(memory_space=pl.ANY)
     scale = math.log2(math.e) / math.sqrt(head_width)
-    return pl.pallas_call(
-        functools.partial(attend_kernel, scale, groups, slice_rows),
-        out_shape=jax.ShapeDtypeStruct(even_query.shape, jnp.bfloat16),
-        in_specs=[vmem] * (4 + len(blocks)),
-        out_specs=vmem,
-        compiler_params=pltpu.CompilerParams(vmem_limit_bytes=24 << 20),
-        cost_estimate=pl.CostEstimate(
+    early = tuple(mask for mask in range(len(blocks)) if mask not in late)
+    state = jax.ShapeDtypeStruct((groups, rows // groups, head_width), jnp.float32)
+    out = jax.ShapeDtypeStruct(shape, jnp.bfloat16)
+    scratch = [pltpu.VMEM(shape, jnp.bfloat16), pltpu.SemaphoreType.DMA((groups,))]
+    params = pltpu.CompilerParams(vmem_limit_bytes=24 << 20)
+    prefix = prefix_len.reshape(1, -1)
+
+    def cost(masks):
+        keys = len(masks) * blocks[0].shape[1]
+        return pl.CostEstimate(
             flops=4 * keys * rows * head_width,
             bytes_accessed=4 * rows * head_width,
             transcendentals=keys * rows,
-        ),
-        name="attend",
-    )(prefix_len.reshape(1, -1), even_query, odd_query, own, *blocks)
+        )
+
+    *partial, begun = pl.pallas_call(
+        functools.partial(early_kernel, scale, groups, early),
+        out_shape=(state, state, state, out),
+        in_specs=[vmem] * (4 + len(early)),
+        out_specs=(vmem, vmem, vmem, hbm),
+        scratch_shapes=scratch,
+        compiler_params=params,
+        cost_estimate=cost(early),
+        name="attend_early",
+    )(prefix, even_query, odd_query, ring, *[blocks[mask] for mask in early])
+    return pl.pallas_call(
+        functools.partial(late_kernel, scale, groups, late),
+        out_shape=out,
+        in_specs=[vmem] * (7 + len(late)) + [hbm],
+        out_specs=hbm,
+        input_output_aliases={7 + len(late): 0},
+        scratch_shapes=scratch,
+        compiler_params=params,
+        cost_estimate=cost(late),
+        name="attend_late",
+    )(prefix, even_query, odd_query, ring, *[blocks[mask] for mask in late], *partial, begun)
 
 
 def block_scores(grouped, key_block, factor):
@@ -186,15 +283,8 @@
 
 def gather_plan(sections):
     every = range(sections)
-    top = sections // 2
-
-    def rank(mask):
-        if mask.bit_count() > 1:
-            return mask.bit_count(), -mask
-        return 1, 0 if mask == top else mask
-
     moves = []
-    for mask in sorted(range(1, sections), key=rank):
+    for mask in sorted(range(1, sections), key=lambda mask: (mask.bit_count(), -mask)):
         swap = [(device, device ^ (mask & -mask)) for device in every]
         moves.append((f"m{mask}", f"m{mask & (mask - 1)}", swap))
     singles = sections.bit_length() - 1
@@ -202,12 +292,13 @@
     ring = [(device, (device + 1) % sections) for device in every]
     onward = [(d, d ^ 2 if d % 2 else (d + 2) % sections) for d in every]
     return [
+        moves[0],
         ("near_query", "query", neighbours),
-        *moves[:singles],
-        ("near_own", "own", ring),
-        *moves[singles:-1],
+        *moves[1:singles],
+        ("ring", "rest", ring),
+        *moves[singles:-2],
         ("even_query", "near_query", onward),
-        moves[-1],
+        *moves[-2:],
     ]
 
 
@@ -221,16 +312,19 @@
     groups = slice_own_keys.shape[1]
     sections = lax.axis_size("pipe")
 
+    own = packed(slice_own_keys, slice_own_values)
+    relayed = queries.shape[0] // 2
+    late = (sections // 2 - 1, sections - 1)
     held = {
-        "query": queries,
-        "own": packed(slice_own_keys, slice_own_values),
+        "query": queries[:relayed],
+        "rest": jnp.concatenate([queries[relayed:], own.reshape(-1, *queries.shape[1:])]),
         "m0": packed(cache_keys, context_value_rows),
     }
     for name, source, pairs in gather_plan(sections):
         held[name] = lax.ppermute(held[source], "pipe", pairs)
     blocks = [held[f"m{mask}"] for mask in range(sections)]
     return attend(
-        prefix_len, held["even_query"], held["near_query"], held["near_own"], blocks, groups
+        prefix_len, held["even_query"], held["near_query"], held["ring"], blocks, late, queries.shape, groups
     )
 
 

time: 31.9 us -> 27.1 us (0.85)
  waiting for transfers between devices: 14.6 us -> 9.53 us
    ppermute x10, waiting for transfers between devices: 14.6 us -> 9.53 us  [swapped_shards(): held[name] = lax.ppermute(held[source], 'pipe', pairs)]
    pallas_call x1 -> x2, Pallas kernels: 1.64 us -> 1.62 us  [the longest x1 1.6 us: attend(): pl.pallas_call(functools.partial(early_kernel, scale, groups, early), out...]
  transfers between devices with their start and end apart: 10 -> 10, of which waited for: 6 -> 6; matrix products, arithmetic and copies ran while one was open for 3% -> 0% of each run, Pallas kernels for 0% -> 6%
where the time goes in v1:
time: 27.1 us; the launch traced here: 27 us
  starting transfers between devices  14.8 us (55%)
  waiting for transfers between devices  9.53 us (35%)
  Pallas kernels  1.62 us (6%)
  local copies, waits for them, and re-layouts  0.94 us (3%)
    ppermute x10, starting transfers between devices, swapped_shards(): held[name] = lax.ppermute(held[source], 'pipe', pairs)  14.8 us
    ppermute x10, waiting for transfers between devices, swapped_shards(): held[name] = lax.ppermute(held[source], 'pipe', pairs)  9.53 us
    pallas_call x1, Pallas kernels, attend(): pl.pallas_call(functools.partial(early_kernel, scale, groups, early), out...  1.6 us
    transpose x2, local copies, waits for them, and re-layouts, packed(): jnp.transpose(values, (1, 0, 2))  0.9 us
  transfers between devices with their start and end apart: 10, of which 6 were waited for; matrix products, arithmetic and copies ran while one was open for 0% of the time, Pallas kernels for 6%

profile of v1, /device:TPU:0, one launch (start us, length us, event | category | flops | bytes accessed | tf_op | source)
XLA Modules:
  0.0 27.0 jit_solution(17486478010657418202)
XLA Ops:
  0.0 0.0 copy-start.1
  0.0 0.9 %copy_bitcast_fusion = (bf16[2,104,128]{2,1,0:T(8,128)(2,1)S(1)}, bf16[2,104,128]{2,1,0:T(8,128)(2,1)S(1)}) fusion(bf16[104,2,128]{2,1,0:T(2,128)(2,1)} %param.10, bf16[104,2,128]{2,1,0:T(2,128)(2,1)} %param.9), kind=kLoop, calls=%fused_computation.2 | loop fusion | bytes 212992 | tf_op jit(solution)/shard_map/transpose | solution.py:306
  0.9 0.0 copy-start.2
  0.9 0.0 copy-start.3
  0.9 4.1 %collective-permute-start.5 = (bf16[4,104,128]{2,1,0:T(8,128)(2,1)S(1)}, bf16[4,104,128]{2,1,0:T(8,128)(2,1)S(1)}, u32[]{:S(2)}, u32[]{:S(2)}) collective-permute-start(bf16[4,104,128]{2,1,0:T(8,128)(2,1)S(1)} %pad_maximum_fusion.1.refs_0_), channel_id=1, source_target_pairs={{0,8},{2,10},{4,12},{6,14},{8,0},{10,2},{12,4},{14,6},{1,9},{3,11}... | collective-permute-start | bytes 319496 | tf_op jit(solution)/shard_map/ppermute | solution.py:324
  5.1 1.6 %collective-permute-start.3 = (bf16[4,104,128]{2,1,0:T(8,128)(2,1)S(1)}, bf16[4,104,128]{2,1,0:T(8,128)(2,1)S(1)}, u32[]{:S(2)}, u32[]{:S(2)}) collective-permute-start(bf16[4,104,128]{2,1,0:T(8,128)(2,1)S(1)} %pad_maximum_fusion.1.refs_0_), channel_id=1, source_target_pairs={{0,4},{2,6},{4,0},{6,2},{8,12},{10,14},{12,8},{14,10},{1,5},{3,7},... | collective-permute-start | bytes 319496 | tf_op jit(solution)/shard_map/ppermute | solution.py:324
  6.7 1.5 %collective-permute-start.8 = (bf16[4,104,128]{2,1,0:T(8,128)(2,1)S(1)}, bf16[4,104,128]{2,1,0:T(8,128)(2,1)S(1)}, u32[]{:S(2)}, u32[]{:S(2)}) collective-permute-start(bf16[4,104,128]{2,1,0:T(8,128)(2,1)S(1)} %pad_maximum_fusion.1.refs_0_), channel_id=1, source_target_pairs={{0,2},{2,0},{4,6},{6,4},{8,10},{10,8},{12,14},{14,12},{1,3},{3,1},... | collective-permute-start | bytes 319496 | tf_op jit(solution)/shard_map/ppermute | solution.py:324
  8.1 0.0 copy-done.1
  8.2 0.6 %collective-permute-start = (bf16[16,32,128]{2,1,0:T(8,128)(2,1)S(1)}, bf16[16,32,128]{2,1,0:T(8,128)(2,1)S(1)}, u32[]{:S(2)}, u32[]{:S(2)}) collective-permute-start(bf16[16,32,128]{2,1,0:T(8,128)(2,1)S(1)} %get-tuple-element.14), channel_id=1, source_target_pairs={{0,2},{2,0},{4,6},{6,4},{8,10},{10,8},{12,14},{14,12},{1,3},{3,1},... | collective-permute-start | bytes 393224 | tf_op jit(solution)/shard_map/ppermute | solution.py:324
  8.8 0.0 copy-done.2
  8.8 0.0 copy-done.3
  8.8 1.6 %collective-permute-done.5.refs_3_ = bf16[4,104,128]{2,1,0:T(8,128)(2,1)S(1)} collective-permute-done((bf16[4,104,128]{2,1,0:T(8,128)(2,1)S(1)}, bf16[4,104,128]{2,1,0:T(8,128)(2,1)S(1)}, u32[]{:S(2)}, u32[]{:S(2)}) %collective-permute-start.5) | collective-permute-done | bytes 106528 | tf_op jit(solution)/shard_map/ppermute | solution.py:324
  10.4 0.6 %collective-permute-start.6 = (bf16[4,104,128]{2,1,0:T(8,128)(2,1)S(1)}, bf16[4,104,128]{2,1,0:T(8,128)(2,1)S(1)}, u32[]{:S(2)}, u32[]{:S(2)}) collective-permute-start(bf16[4,104,128]{2,1,0:T(8,128)(2,1)S(1)} %collective-permute-done.5.refs_3_), channel_id=1, source_target_pairs={{0,4},{2,6},{4,0},{6,2},{8,12},{10,14},{12,8},{14,10},{1,5},{3,7},... | collective-permute-start | bytes 319496 | tf_op jit(solution)/shard_map/ppermute | solution.py:324
  11.1 0.0 copy-start
  11.1 1.5 %collective-permute-start.2 = (bf16[20,32,128]{2,1,0:T(8,128)(2,1)S(1)}, bf16[20,32,128]{2,1,0:T(8,128)(2,1)S(1)}, u32[]{:S(2)}, u32[]{:S(2)}) collective-permute-start(bf16[20,32,128]{2,1,0:T(8,128)(2,1)S(1)} %pad_maximum_fusion), channel_id=1, source_target_pairs={{0,2},{2,4},{4,6},{6,8},{8,10},{10,12},{12,14},{14,0},{1,3},{3,5},... | collective-permute-start | bytes 491528 | tf_op jit(solution)/shard_map/ppermute | solution.py:324
  12.6 1.1 %collective-permute-done.odd_ref = bf16[16,32,128]{2,1,0:T(8,128)(2,1)S(1)} collective-permute-done((bf16[16,32,128]{2,1,0:T(8,128)(2,1)S(1)}, bf16[16,32,128]{2,1,0:T(8,128)(2,1)S(1)}, u32[]{:S(2)}, u32[]{:S(2)}) %collective-permute-start) | collective-permute-done | bytes 131104 | tf_op jit(solution)/shard_map/ppermute | solution.py:324
  13.8 0.4 %collective-permute-start.1 = (bf16[16,32,128]{2,1,0:T(8,128)(2,1)S(1)}, bf16[16,32,128]{2,1,0:T(8,128)(2,1)S(1)}, u32[]{:S(2)}, u32[]{:S(2)}) collective-permute-start(bf16[16,32,128]{2,1,0:T(8,128)(2,1)S(1)} %collective-permute-done.odd_ref), channel_id=1, source_target_pairs={{0,4},{2,6},{4,8},{6,2},{8,12},{10,14},{12,0},{14,10},{1,5},{3,7},... | collective-permute-start | bytes 393224 | tf_op jit(solution)/shard_map/ppermute | solution.py:324
  14.2 0.0 collective-permute-done.3.refs_2_
  14.2 2.3 %collective-permute-start.9 = (bf16[4,104,128]{2,1,0:T(8,128)(2,1)S(1)}, bf16[4,104,128]{2,1,0:T(8,128)(2,1)S(1)}, u32[]{:S(2)}, u32[]{:S(2)}) collective-permute-start(bf16[4,104,128]{2,1,0:T(8,128)(2,1)S(1)} %collective-permute-done.5.refs_3_), channel_id=1, source_target_pairs={{0,2},{2,0},{4,6},{6,4},{8,10},{10,8},{12,14},{14,12},{1,3},{3,1},... | collective-permute-start | bytes 319496 | tf_op jit(solution)/shard_map/ppermute | solution.py:324
  16.6 0.0 collective-permute-done.8.refs_1_
  16.6 0.1 collective-permute-start.4
  16.6 0.0 collective-permute-done.6.refs_5_
  16.6 2.0 %collective-permute-start.7 = (bf16[4,104,128]{2,1,0:T(8,128)(2,1)S(1)}, bf16[4,104,128]{2,1,0:T(8,128)(2,1)S(1)}, u32[]{:S(2)}, u32[]{:S(2)}) collective-permute-start(bf16[4,104,128]{2,1,0:T(8,128)(2,1)S(1)} %collective-permute-done.6.refs_5_), channel_id=1, source_target_pairs={{0,2},{2,0},{4,6},{6,4},{8,10},{10,8},{12,14},{14,12},{1,3},{3,1},... | collective-permute-start | bytes 319496 | tf_op jit(solution)/shard_map/ppermute | solution.py:324
  18.6 3.5 %collective-permute-done.2.ring_ref = bf16[20,32,128]{2,1,0:T(8,128)(2,1)S(1)} collective-permute-done((bf16[20,32,128]{2,1,0:T(8,128)(2,1)S(1)}, bf16[20,32,128]{2,1,0:T(8,128)(2,1)S(1)}, u32[]{:S(2)}, u32[]{:S(2)}) %collective-permute-start.2) | collective-permute-done | bytes 163872 | tf_op jit(solution)/shard_map/ppermute | solution.py:324
  22.1 1.3 %collective-permute-done.9.refs_4_ = bf16[4,104,128]{2,1,0:T(8,128)(2,1)S(1)} collective-permute-done((bf16[4,104,128]{2,1,0:T(8,128)(2,1)S(1)}, bf16[4,104,128]{2,1,0:T(8,128)(2,1)S(1)}, u32[]{:S(2)}, u32[]{:S(2)}) %collective-permute-start.9) | collective-permute-done | bytes 106528 | tf_op jit(solution)/shard_map/ppermute | solution.py:324
  23.5 0.0 collective-permute-done.1.even_ref
  23.5 0.0 copy-done
  23.5 1.6 %attend_early.1 = (f32[2,512,128]{2,1,0:T(8,128)S(1)}, f32[2,512,128]{2,1,0:T(8,128)S(1)}, f32[2,512,128]{2,1,0:T(8,128)S(1)}, bf16[32,32,128]{2,1,0:T(8,128)(2,1)}) custom-call(s32[1,8]{1,0:T(1,128)S(1)} %bitcast.9, bf16[16,32,128]{2,1,0:T(8,128)(2,1)S(1)} %collective-permute-done.1.even_ref, bf16[16,32,128]{2,1,0:T(8,128)(2,1)S(1)} %collective-permute-done.odd_ref, ...), custom_call_target="tpu_custom_call" | custom-call | flops 327155712 | bytes 524288 | tf_op jit(solution)/shard_map/attend_early/pallas_call | solution.py:182
  25.1 0.7 %collective-permute-done.4.refs_0_ = bf16[4,104,128]{2,1,0:T(8,128)(2,1)S(1)} collective-permute-done((bf16[4,104,128]{2,1,0:T(8,128)(2,1)S(1)}, bf16[4,104,128]{2,1,0:T(8,128)(2,1)S(1)}, u32[]{:S(2)}, u32[]{:S(2)}) %collective-permute-start.4) | collective-permute-done | bytes 106528 | tf_op jit(solution)/shard_map/ppermute | solution.py:324
  25.8 1.2 %collective-permute-done.7.refs_1_ = bf16[4,104,128]{2,1,0:T(8,128)(2,1)S(1)} collective-permute-done((bf16[4,104,128]{2,1,0:T(8,128)(2,1)S(1)}, bf16[4,104,128]{2,1,0:T(8,128)(2,1)S(1)}, u32[]{:S(2)}, u32[]{:S(2)}) %collective-permute-start.7) | collective-permute-done | bytes 106528 | tf_op jit(solution)/shard_map/ppermute | solution.py:324
  (5 shorter events, 0.1 us)
Async XLA Ops:
  0.0 8.1 %copy-start.1 = (bf16[32,32,128]{2,1,0:T(8,128)(2,1)S(1)}, bf16[32,32,128]{2,1,0:T(8,128)(2,1)}, u32[]{:S(2)}) copy-start(bf16[32,32,128]{2,1,0:T(8,128)(2,1)} %param.6) | copy-start | bytes 786436
  0.9 7.8 %copy-start.2 = (bf16[32,2,128]{2,1,0:T(2,128)(2,1)S(1)}, bf16[32,2,128]{2,1,0:T(2,128)(2,1)}, u32[]{:S(2)}) copy-start(bf16[32,2,128]{2,1,0:T(2,128)(2,1)} %param.8) | copy-start | bytes 49156
  0.9 7.8 %copy-start.3 = (bf16[32,2,128]{2,1,0:T(2,128)(2,1)S(1)}, bf16[32,2,128]{2,1,0:T(2,128)(2,1)}, u32[]{:S(2)}) copy-start(bf16[32,2,128]{2,1,0:T(2,128)(2,1)} %param.7) | copy-start | bytes 49156
  0.9 9.5 %collective-permute-start.5 = (bf16[4,104,128]{2,1,0:T(8,128)(2,1)S(1)}, bf16[4,104,128]{2,1,0:T(8,128)(2,1)S(1)}, u32[]{:S(2)}, u32[]{:S(2)}) collective-permute-start(bf16[4,104,128]{2,1,0:T(8,128)(2,1)S(1)} %pad_maximum_fusion.1.refs_0_), channel_id=1, source_target_pairs={{0,8},{2,10},{4,12},{6,14},{8,0},{10,2},{12,4},{14,6},{1,9},{3,11}... | collective-permute-start | bytes 319496 | tf_op jit(solution)/shard_map/ppermute | solution.py:324
  5.1 9.1 %collective-permute-start.3 = (bf16[4,104,128]{2,1,0:T(8,128)(2,1)S(1)}, bf16[4,104,128]{2,1,0:T(8,128)(2,1)S(1)}, u32[]{:S(2)}, u32[]{:S(2)}) collective-permute-start(bf16[4,104,128]{2,1,0:T(8,128)(2,1)S(1)} %pad_maximum_fusion.1.refs_0_), channel_id=1, source_target_pairs={{0,4},{2,6},{4,0},{6,2},{8,12},{10,14},{12,8},{14,10},{1,5},{3,7},... | collective-permute-start | bytes 319496 | tf_op jit(solution)/shard_map/ppermute | solution.py:324
  6.7 9.9 %collective-permute-start.8 = (bf16[4,104,128]{2,1,0:T(8,128)(2,1)S(1)}, bf16[4,104,128]{2,1,0:T(8,128)(2,1)S(1)}, u32[]{:S(2)}, u32[]{:S(2)}) collective-permute-start(bf16[4,104,128]{2,1,0:T(8,128)(2,1)S(1)} %pad_maximum_fusion.1.refs_0_), channel_id=1, source_target_pairs={{0,2},{2,0},{4,6},{6,4},{8,10},{10,8},{12,14},{14,12},{1,3},{3,1},... | collective-permute-start | bytes 319496 | tf_op jit(solution)/shard_map/ppermute | solution.py:324
  8.2 5.6 %collective-permute-start = (bf16[16,32,128]{2,1,0:T(8,128)(2,1)S(1)}, bf16[16,32,128]{2,1,0:T(8,128)(2,1)S(1)}, u32[]{:S(2)}, u32[]{:S(2)}) collective-permute-start(bf16[16,32,128]{2,1,0:T(8,128)(2,1)S(1)} %get-tuple-element.14), channel_id=1, source_target_pairs={{0,2},{2,0},{4,6},{6,4},{8,10},{10,8},{12,14},{14,12},{1,3},{3,1},... | collective-permute-start | bytes 393224 | tf_op jit(solution)/shard_map/ppermute | solution.py:324
  10.4 6.2 %collective-permute-start.6 = (bf16[4,104,128]{2,1,0:T(8,128)(2,1)S(1)}, bf16[4,104,128]{2,1,0:T(8,128)(2,1)S(1)}, u32[]{:S(2)}, u32[]{:S(2)}) collective-permute-start(bf16[4,104,128]{2,1,0:T(8,128)(2,1)S(1)} %collective-permute-done.5.refs_3_), channel_id=1, source_target_pairs={{0,4},{2,6},{4,0},{6,2},{8,12},{10,14},{12,8},{14,10},{1,5},{3,7},... | collective-permute-start | bytes 319496 | tf_op jit(solution)/shard_map/ppermute | solution.py:324
  11.1 12.4 %copy-start = (s32[8]{0:T(128)S(1)}, s32[8]{0:T(128)}, u32[]{:S(2)}) copy-start(s32[8]{0:T(128)} %param.11) | copy-start | bytes 100
  11.1 11.0 %collective-permute-start.2 = (bf16[20,32,128]{2,1,0:T(8,128)(2,1)S(1)}, bf16[20,32,128]{2,1,0:T(8,128)(2,1)S(1)}, u32[]{:S(2)}, u32[]{:S(2)}) collective-permute-start(bf16[20,32,128]{2,1,0:T(8,128)(2,1)S(1)} %pad_maximum_fusion), channel_id=1, source_target_pairs={{0,2},{2,4},{4,6},{6,8},{8,10},{10,12},{12,14},{14,0},{1,3},{3,5},... | collective-permute-start | bytes 491528 | tf_op jit(solution)/shard_map/ppermute | solution.py:324
  13.8 9.7 %collective-permute-start.1 = (bf16[16,32,128]{2,1,0:T(8,128)(2,1)S(1)}, bf16[16,32,128]{2,1,0:T(8,128)(2,1)S(1)}, u32[]{:S(2)}, u32[]{:S(2)}) collective-permute-start(bf16[16,32,128]{2,1,0:T(8,128)(2,1)S(1)} %collective-permute-done.odd_ref), channel_id=1, source_target_pairs={{0,4},{2,6},{4,8},{6,2},{8,12},{10,14},{12,0},{14,10},{1,5},{3,7},... | collective-permute-start | bytes 393224 | tf_op jit(solution)/shard_map/ppermute | solution.py:324
  14.2 9.2 %collective-permute-start.9 = (bf16[4,104,128]{2,1,0:T(8,128)(2,1)S(1)}, bf16[4,104,128]{2,1,0:T(8,128)(2,1)S(1)}, u32[]{:S(2)}, u32[]{:S(2)}) collective-permute-start(bf16[4,104,128]{2,1,0:T(8,128)(2,1)S(1)} %collective-permute-done.5.refs_3_), channel_id=1, source_target_pairs={{0,2},{2,0},{4,6},{6,4},{8,10},{10,8},{12,14},{14,12},{1,3},{3,1},... | collective-permute-start | bytes 319496 | tf_op jit(solution)/shard_map/ppermute | solution.py:324
  16.6 9.2 %collective-permute-start.4 = (bf16[4,104,128]{2,1,0:T(8,128)(2,1)S(1)}, bf16[4,104,128]{2,1,0:T(8,128)(2,1)S(1)}, u32[]{:S(2)}, u32[]{:S(2)}) collective-permute-start(bf16[4,104,128]{2,1,0:T(8,128)(2,1)S(1)} %collective-permute-done.3.refs_2_), channel_id=1, source_target_pairs={{0,2},{2,0},{4,6},{6,4},{8,10},{10,8},{12,14},{14,12},{1,3},{3,1},... | collective-permute-start | bytes 319496 | tf_op jit(solution)/shard_map/ppermute | solution.py:324
  16.6 10.3 %collective-permute-start.7 = (bf16[4,104,128]{2,1,0:T(8,128)(2,1)S(1)}, bf16[4,104,128]{2,1,0:T(8,128)(2,1)S(1)}, u32[]{:S(2)}, u32[]{:S(2)}) collective-permute-start(bf16[4,104,128]{2,1,0:T(8,128)(2,1)S(1)} %collective-permute-done.6.refs_5_), channel_id=1, source_target_pairs={{0,2},{2,0},{4,6},{6,4},{8,10},{10,8},{12,14},{14,12},{1,3},{3,1},... | collective-permute-start | bytes 319496 | tf_op jit(solution)/shard_map/ppermute | solution.py:324
